TPU v7x, 32 devices: a whole 2x2x4 slice. The times are simulated.
32 devices in a mesh: group: 2 (over y), expert: 4 (over z), dp: 4 (over x, core).
Axes of the slice: x: 2, y: 2, z: 4, core: 2. Of those that a mesh axis runs over, the one named last changes fastest.
Arguments:
- tokens: bfloat16 [256, 4096], P(('group', 'expert', 'dp')), parts along dimension 0, may hold values from -6 to 6
- routing: int32 [256, 8], P(('group', 'expert', 'dp')), parts along dimension 0, may hold values from 0 to 127, as said below
- gate_quantized: int32 [256, 8], P(('group', 'expert', 'dp')), parts along dimension 0, may hold values from 1 to 32767
- tenant: int32 [256], P(('group', 'expert', 'dp')), parts along dimension 0, may hold values from 0 to 23
- tenant_page_lookup: int32 [4, 24], replicated, may hold values from 0 to 23, each once within a row
- gate_weight: bfloat16 [4, 4096, 1024], P('expert', None, 'dp'), may hold values from -0.09375 to 0.09375
- up_projection: bfloat16 [4, 4096, 1024], P('expert', None, 'dp'), may hold values from -0.09375 to 0.09375
- down_weight: bfloat16 [4, 1024, 4096], P('expert', None, 'dp'), may hold values from -0.1875 to 0.1875
- adapter_shrink: bfloat16 [4, 24, 16, 4096], P('expert', 'dp'), may hold values from -0.09375 to 0.09375
- adapter_expand: bfloat16 [4, 24, 16, 1024], P('expert', 'dp'), may hold values from -1.5 to 1.5
Outputs:
- mixed_out: bfloat16 [256, 4096], P(('group', 'expert', 'dp')), parts along dimension 0
There are 2 independent parts, one for each index of `group`. A program takes and returns all parts, laid end to end along the dimension named above; an argument that names none is the same for every part. Nothing has to cross between parts.
Inputs may be any that keep to these rules, and one draw needn't show every extreme that they name: `routing`: each row names 8 different experts. Among the 8 tokens of one device no expert is named more than 2 times, and in every draw some expert below 4 is named exactly 2 times by the tokens of every device. `tenant_page_lookup`: row e gives every tenant a different page of expert e's pool.
All inputs are finite; a program needn't handle non-finite values.
Results may differ from a plain program's by a relative error of at most 0.0061.
Values may be sent and summed in bfloat16 or wider, within the bound.
A program may use at most 64 MiB of HBM per device.

v0:
```python
import jax
import jax.numpy as jnp
from jax import lax
from jax.sharding import PartitionSpec as P


def slot_tables(routing, experts, capacity):
    expert_ids = jnp.arange(experts, dtype=jnp.int32)
    matches = routing[:, :, None] == expert_ids[None, None, :]
    assign = jnp.sum(matches.astype(jnp.int32), axis=1)
    slot_rank = jnp.cumsum(assign, axis=0) - assign
    scale_levels = jnp.arange(capacity, dtype=jnp.int32)
    placing = (assign.T[:, None, :] == 1) & (slot_rank.T[:, None, :] == scale_levels[None, :, None])
    return (matches, slot_rank, placing)


def per_device(
    tokens,
    routing,
    gate_quantized,
    tenant,
    tenant_page_lookup,
    gate_weight,
    up_projection,
    down_weight,
    adapter_shrink,
    adapter_expand,
):
    tok_count, model_width = tokens.shape
    experts, tenants = tenant_page_lookup.shape
    capacity = tok_count // 4
    rank_extent = adapter_shrink.shape[2]
    part_width = down_weight.shape[2]
    my_expert = lax.axis_index("expert")
    matches, slot_rank, placing = slot_tables(routing, experts, capacity)
    send_rows = jnp.einsum(
        "ect,td->ecd", placing.astype(jnp.bfloat16), tokens, preferred_element_type=jnp.float32
    ).astype(jnp.bfloat16)
    send_ten = jnp.sum(placing.astype(jnp.int32) * (tenant[None, None, :] + 1), axis=2)
    got_rows, got_ten = (
        lax.all_to_all(send_rows, "expert", split_axis=0, concat_axis=0, tiled=True),
        lax.all_to_all(send_ten, "expert", split_axis=0, concat_axis=0, tiled=True),
    )
    slot_rows, slot_ten = (
        lax.all_gather(got_rows[None], "dp", axis=0, tiled=True),
        lax.all_gather(got_ten[None], "dp", axis=0, tiled=True),
    )
    block_shape = slot_rows.shape[:3]
    slot_count = block_shape[0] * block_shape[1] * block_shape[2]
    slot_input = slot_rows.reshape(slot_count, model_width)
    slot_tenant = slot_ten.reshape(slot_count)
    page_row = lax.dynamic_index_in_dim(tenant_page_lookup, my_expert, 0, keepdims=False)
    tenant_ids = jnp.arange(tenants, dtype=jnp.int32)
    tenant_hot = slot_tenant[:, None] == tenant_ids[None, :] + 1
    slot_page = jnp.sum(jnp.where(tenant_hot, page_row[None, :], 0), axis=1)
    occupied = slot_tenant > 0
    page_pick = ((slot_page[:, None] == tenant_ids[None, :]) & occupied[:, None]).astype(
        jnp.float32
    )
    partial_terms = lax.all_gather(adapter_shrink, "dp", axis=1, tiled=True)
    page_count = partial_terms.shape[1]
    flat_pages = partial_terms.reshape(page_count * rank_extent, model_width)
    products = lax.dot_general(
        slot_input, flat_pages, (((1,), (1,)), ((), ())), preferred_element_type=jnp.float32
    )
    shrink_result = jnp.sum(
        page_pick[:, :, None] * products.reshape(slot_count, page_count, rank_extent), axis=1
    )
    shrink_low = shrink_result.astype(jnp.bfloat16)
    expand_every_page = lax.all_to_all(
        adapter_expand, "dp", split_axis=3, concat_axis=1, tiled=True
    )[0]
    hidden_part = expand_every_page.shape[2]
    expand_matrix = expand_every_page.reshape(tenants * rank_extent, hidden_part)
    spread_rows = (page_pick[:, :, None] * shrink_low.astype(jnp.float32)[:, None, :]).astype(
        jnp.bfloat16
    )
    spread_rows = spread_rows.reshape(slot_count, tenants * rank_extent)
    adapter_update = jnp.dot(spread_rows, expand_matrix, preferred_element_type=jnp.float32)
    gate_act = jnp.dot(slot_input, gate_weight[0], preferred_element_type=jnp.float32)
    up_activation = (
        jnp.dot(slot_input, up_projection[0], preferred_element_type=jnp.float32) + adapter_update
    )
    hidden = (jax.nn.silu(gate_act) * up_activation).astype(jnp.bfloat16)
    weights = down_weight[0]
    expert_out = jnp.dot(
        lax.all_gather(hidden, "dp", axis=1, tiled=True),
        weights,
        preferred_element_type=jnp.float32,
    )
    expert_out = expert_out.astype(jnp.bfloat16).reshape(block_shape + (part_width,))
    home_rows = lax.all_to_all(expert_out, "dp", split_axis=0, concat_axis=3, tiled=True)
    back_rows = lax.all_to_all(home_rows, "expert", split_axis=1, concat_axis=0, tiled=True)
    back_rows = back_rows.reshape(experts * capacity, model_width)
    chosen_rank = jnp.sum(jnp.where(matches, slot_rank[:, None, :], 0), axis=2)
    inside = routing < experts
    flat_index = routing * capacity + chosen_rank
    slot_ids = jnp.arange(experts * capacity, dtype=jnp.int32)
    row_picks = ((flat_index[:, :, None] == slot_ids[None, None, :]) & inside[:, :, None]).astype(
        jnp.bfloat16
    )
    picked = jnp.einsum("tkm,md->tkd", row_picks, back_rows, preferred_element_type=jnp.float32)
    mix_coef = jnp.where(inside, gate_quantized.astype(jnp.float32) / 32768.0, jnp.float32(0.0))
    mixed_out = jnp.sum(mix_coef[:, :, None] * picked, axis=1)
    return mixed_out.astype(jnp.bfloat16)


def solution(mesh):
    return jax.shard_map(
        per_device,
        mesh=mesh,
        in_specs=(
            P(("group", "expert", "dp"), None),
            P(("group", "expert", "dp"), None),
            P(("group", "expert", "dp"), None),
            P(("group", "expert", "dp")),
            P(),
            P("expert", None, "dp"),
            P("expert", None, "dp"),
            P("expert", None, "dp"),
            P("expert", "dp", None, None),
            P("expert", "dp", None, None),
        ),
        out_specs=P(("group", "expert", "dp"), None),
        check_vma=False,
    )
```

profile of v0, /device:TPU:0, one launch (start us, length us, event | category | flops | bytes accessed | tf_op | source)
XLA Modules:
  0.0 94.2 jit_solution(14872100671156031645)
XLA Ops:
  6.5 0.0 copy-start
  6.5 0.0 all-gather.4.cloned.1.call-start
  6.5 0.7 all-gather.4.cloned.1.call-update
  7.3 0.8 convert_reduce_fusion
  8.1 0.2 reduce_window_sum.11
  8.3 0.7 broadcast_add_fusion
  9.0 0.1 select_reduce_fusion.2
  9.1 0.7 copy.39
  9.8 6.3 %all-to-all-start.1 = ((s32[4,1,2]{2,1,0:T(1,128)}), s32[4,1,2]{2,1,0:T(1,128)S(1)}, u32[]{:S(2)}, u32[]{:S(2)}) async-start(s32[4,1,2]{2,1,0:T(1,128)} %copy.39), calls=%async_computation.1 | async-start | bytes 4096 | tf_op jit(solution)/shard_map/all_to_all | solution.py:42
  16.1 1.0 %convolution_convert_fusion = bf16[4,2,4096]{2,0,1:T(4,128)(2,1)S(1)} fusion(bf16[8,4096]{1,0:T(8,128)(2,1)} %param.10, s32[4,8]{1,0:T(4,128)S(1)} %bitcast.58, pred[4,8]{1,0:T(4,128)(4,1)S(1)} %compare_bitcast_fusion), kind=kOutput, calls=%fused_computation.1 | convolution fusion | flops 557184 | bytes 131232 | tf_op jit(solution)/shard_map/ect,td->ecd/dot_general | solution.py:36
  17.1 0.7 copy.38
  17.8 3.3 %copy.43 = bf16[1,6,16,1024]{2,1,0,3:T(8,128)(2,1)} copy(bf16[1,6,16,1024]{3,2,1,0:T(8,128)(2,1)} %param.19) | data formatting | bytes 393216 | tf_op args[9]
  21.2 3.5 %reshape.122 = bf16[4,2,12288]{2,1,0:T(2,128)(2,1)} reshape(bf16[1024,1,6,16]{3,2,1,0:T(8,128)(2,1)} %bitcast.51) | data formatting | bytes 393216
  24.7 0.7 dynamic-slice_bitcast_fusion
  25.4 0.0 copy-done.2
  25.4 0.0 copy-done.3
  25.4 0.0 all-to-all-done.1
  25.4 5.1 %all-to-all-start = ((bf16[4,2,4096]{2,1,0:T(2,128)(2,1)}), bf16[4,2,4096]{2,1,0:T(2,128)(2,1)S(1)}, u32[]{:S(2)}, u32[]{:S(2)}) async-start(bf16[4,2,4096]{2,1,0:T(2,128)(2,1)} %copy.38), calls=%async_computation | async-start | bytes 131072 | tf_op jit(solution)/shard_map/all_to_all | solution.py:41
  30.5 5.3 %all-gather.1 = s32[16,1,2]{2,1,0:T(1,128)S(1)} all-gather(s32[4,1,2]{2,1,0:T(1,128)S(1)} %all-to-all-done.1), channel_id=3, replica_groups=mesh['group'=2,'expert'=4,'dp'=4] {'dp'}, dimensions={0}, use_global_device_ids=true | all-gather | bytes 160 | tf_op jit(solution)/shard_map/all_gather | solution.py:46
  35.8 0.5 broadcast.74
  36.3 0.6 reduce.3
  36.9 0.1 eq.93
  37.0 0.1 select_reduce_fusion.1
  37.1 0.0 all-to-all-done
  37.1 3.4 %all-to-all-start.2 = ((bf16[4,2,12288]{2,1,0:T(2,128)(2,1)}), bf16[4,2,12288]{2,1,0:T(2,128)(2,1)S(1)}, u32[]{:S(2)}, u32[]{:S(2)}) async-start(bf16[4,2,12288]{2,1,0:T(2,128)(2,1)} %reshape.122), calls=%async_computation.2 | async-start | bytes 393216 | tf_op jit(solution)/shard_map/all_to_all | solution.py:70
  40.5 7.5 %all-gather = bf16[16,2,4096]{2,1,0:T(2,128)(2,1)S(1)} all-gather(bf16[4,2,4096]{2,1,0:T(2,128)(2,1)S(1)} %all-to-all-done), channel_id=2, replica_groups=mesh['group'=2,'expert'=4,'dp'=4] {'dp'}, dimensions={0}, use_global_device_ids=true | all-gather | bytes 327680 | tf_op jit(solution)/shard_map/all_gather | solution.py:45
  48.0 0.1 reshape.109
  48.1 0.1 reshape.101
  48.2 0.0 copy-start.1
  48.2 2.2 %fusion.5 = f32[32,256]{1,0:T(8,128)S(1)} fusion(bf16[32,4096]{1,0:T(8,128)(2,1)S(1)} %reshape.101, bf16[1,4096,256]{2,1,0:T(8,128)(2,1)} %param.16), kind=kOutput, calls=%fused_computation.7 | convolution fusion | flops 67108864 | bytes 2392064 | tf_op jit(solution)/shard_map/dot_general | solution.py:82
  50.4 0.0 copy-done.1
  50.5 0.5 fusion.7
  50.9 0.0 all-to-all-done.2
  50.9 2.9 %reshape.123 = bf16[1024,1,6,16]{3,2,1,0:T(8,128)(2,1)} reshape(bf16[4,2,12288]{2,1,0:T(2,128)(2,1)S(1)} %all-to-all-done.2) | data formatting | bytes 393216
  53.9 2.5 %copy.48 = bf16[1,6,16,4,256]{4,3,2,1,0:T(4,128)(2,1)S(1)} copy(bf16[1,6,16,4,256]{2,1,4,3,0:T(8,128)(2,1)} %bitcast.50) | data formatting | bytes 393216 | tf_op jit(solution)/shard_map/all_to_all | solution.py:70
  56.4 0.0 all-gather.4.cloned.1.call-done
  56.4 4.2 %fusion.16 = bf16[32,16]{0,1:T(8,128)(2,1)S(1)} fusion(bf16[32,4096,1]{1,0,2:T(8,128)(2,1)S(1)} %reshape.109, bf16[1,24,16,4096]{3,2,0,1:T(8,128)(2,1)} %all-gather.4.cloned.1.call-done, f32[32,24]{0,1:T(8,128)S(1)} %fusion.27), kind=kOutput, calls=%fused_computation.14 | convolution fusion | flops 100687360 | bytes 3411968 | tf_op jit(solution)/shard_map/dot_general | solution.py:63
  60.7 0.2 fusion.20
  60.9 5.2 %all_gather.15 = bf16[32,1024]{1,0:T(8,128)(2,1)S(1)} all-gather(bf16[32,256]{1,0:T(8,128)(2,1)S(1)} %fusion.20), channel_id=1, replica_groups=mesh['group'=2,'expert'=4,'dp'=4] {'dp'}, dimensions={1}, use_global_device_ids=true | all-gather | bytes 81920 | tf_op jit(solution)/shard_map/all_gather | solution.py:87
  66.2 0.5 fusion.13
  66.6 0.7 reshape.102
  67.3 3.3 %all-to-all-start.3 = ((bf16[4,4,2,1024]{3,2,1,0:T(2,128)(2,1)}), bf16[4,4,2,1024]{3,2,1,0:T(2,128)(2,1)S(1)}, u32[]{:S(2)}, u32[]{:S(2)}) async-start(bf16[4,4,2,1024]{3,2,1,0:T(2,128)(2,1)} %reshape.102), calls=%async_computation.3 | async-start | bytes 131072 | tf_op jit(solution)/shard_map/all_to_all | solution.py:92
  70.6 0.1 select_reduce_fusion
  70.7 4.0 %all-to-all-done.3 = bf16[4,4,2,1024]{3,2,1,0:T(2,128)(2,1)S(1)} async-done(((bf16[4,4,2,1024]{3,2,1,0:T(2,128)(2,1)}), bf16[4,4,2,1024]{3,2,1,0:T(2,128)(2,1)S(1)}, u32[]{:S(2)}, u32[]{:S(2)}) %all-to-all-start.3) | async-done | bytes 65568 | tf_op jit(solution)/shard_map/all_to_all | solution.py:92
  74.7 0.7 copy.49
  75.4 5.1 %all-to-all-start.4 = ((bf16[1,4,2,4096]{3,2,0,1:T(2,128)(2,1)}), bf16[1,4,2,4096]{3,2,0,1:T(2,128)(2,1)S(1)}, u32[]{:S(2)}, u32[]{:S(2)}) async-start(bf16[1,4,2,4096]{3,2,0,1:T(2,128)(2,1)} %bitcast.16), calls=%async_computation.4 | async-start | bytes 131072 | tf_op jit(solution)/shard_map/all_to_all | solution.py:93
  80.5 5.7 %all-to-all-done.4 = bf16[1,4,2,4096]{3,2,0,1:T(2,128)(2,1)S(1)} async-done(((bf16[1,4,2,4096]{3,2,0,1:T(2,128)(2,1)}), bf16[1,4,2,4096]{3,2,0,1:T(2,128)(2,1)S(1)}, u32[]{:S(2)}, u32[]{:S(2)}) %all-to-all-start.4) | async-done | bytes 65568 | tf_op jit(solution)/shard_map/all_to_all | solution.py:93
  86.2 1.1 %fusion.9 = bf16[8,4096]{1,0:T(8,128)(2,1)} fusion(bf16[8,4096,1]{1,0,2:T(8,128)(2,1)S(1)} %reshape.110, f32[8,8]{1,0:T(8,128)S(1)} %get-tuple-element.5, s32[8,8]{1,0:T(8,128)S(1)} %multiply_add_fusion, pred[8,8]{1,0:T(8,128)(4,1)S(1)} %get-tuple-element.6), kind=kOutput, calls=%fused_computation.11 | convolution fusion | flops 4686848 | bytes 131648 | tf_op jit(solution)/shard_map/tkm,md->tkd/dot_general | solution.py:102
  (15 shorter events, 0.1 us)
Async XLA Ops:
  6.5 59.6 %copy-start = (bf16[1,1024,1024]{2,1,0:T(8,128)(2,1)S(1)}, bf16[1,1024,1024]{2,1,0:T(8,128)(2,1)}, u32[]{:S(2)}) copy-start(bf16[1,1024,1024]{2,1,0:T(8,128)(2,1)} %param.17) | copy-start | bytes 6291460
  6.5 49.9 %all-gather.4.cloned.1.call-start = ((), (), s32[]{:S(2)}) async-start(), calls=%async_computation.5 | async-start | bytes 3932160 | tf_op jit(solution)/shard_map/all_gather | solution.py:60
  9.8 15.6 %all-to-all-start.1 = ((s32[4,1,2]{2,1,0:T(1,128)}), s32[4,1,2]{2,1,0:T(1,128)S(1)}, u32[]{:S(2)}, u32[]{:S(2)}) async-start(s32[4,1,2]{2,1,0:T(1,128)} %copy.39), calls=%async_computation.1 | async-start | bytes 4096 | tf_op jit(solution)/shard_map/all_to_all | solution.py:42
  17.8 7.6 %copy-start.2 = (s32[8,8]{1,0:T(8,128)S(1)}, s32[8,8]{1,0:T(8,128)}, u32[]{:S(2)}) copy-start(s32[8,8]{1,0:T(8,128)} %param.11) | copy-start | bytes 772
  17.8 7.6 %copy-start.3 = (s32[8,8]{1,0:T(8,128)S(1)}, s32[8,8]{1,0:T(8,128)}, u32[]{:S(2)}) copy-start(s32[8,8]{1,0:T(8,128)} %param.12) | copy-start | bytes 772
  25.4 11.7 %all-to-all-start = ((bf16[4,2,4096]{2,1,0:T(2,128)(2,1)}), bf16[4,2,4096]{2,1,0:T(2,128)(2,1)S(1)}, u32[]{:S(2)}, u32[]{:S(2)}) async-start(bf16[4,2,4096]{2,1,0:T(2,128)(2,1)} %copy.38), calls=%async_computation | async-start | bytes 131072 | tf_op jit(solution)/shard_map/all_to_all | solution.py:41
  37.1 13.8 %all-to-all-start.2 = ((bf16[4,2,12288]{2,1,0:T(2,128)(2,1)}), bf16[4,2,12288]{2,1,0:T(2,128)(2,1)S(1)}, u32[]{:S(2)}, u32[]{:S(2)}) async-start(bf16[4,2,12288]{2,1,0:T(2,128)(2,1)} %reshape.122), calls=%async_computation.2 | async-start | bytes 393216 | tf_op jit(solution)/shard_map/all_to_all | solution.py:70
  48.2 2.2 %copy-start.1 = (bf16[1,4096,256]{2,1,0:T(8,128)(2,1)S(1)}, bf16[1,4096,256]{2,1,0:T(8,128)(2,1)}, u32[]{:S(2)}) copy-start(bf16[1,4096,256]{2,1,0:T(8,128)(2,1)} %param.15) | copy-start | bytes 6291460
  67.3 7.4 %all-to-all-start.3 = ((bf16[4,4,2,1024]{3,2,1,0:T(2,128)(2,1)}), bf16[4,4,2,1024]{3,2,1,0:T(2,128)(2,1)S(1)}, u32[]{:S(2)}, u32[]{:S(2)}) async-start(bf16[4,4,2,1024]{3,2,1,0:T(2,128)(2,1)} %reshape.102), calls=%async_computation.3 | async-start | bytes 131072 | tf_op jit(solution)/shard_map/all_to_all | solution.py:92
  75.4 10.8 %all-to-all-start.4 = ((bf16[1,4,2,4096]{3,2,0,1:T(2,128)(2,1)}), bf16[1,4,2,4096]{3,2,0,1:T(2,128)(2,1)S(1)}, u32[]{:S(2)}, u32[]{:S(2)}) async-start(bf16[1,4,2,4096]{3,2,0,1:T(2,128)(2,1)} %bitcast.16), calls=%async_computation.4 | async-start | bytes 131072 | tf_op jit(solution)/shard_map/all_to_all | solution.py:93
Sparse Core Ops, SparseCore 0:
  8.9 31.2 all-gather.3
where the time goes:
time: 95 us; the launch traced here: 94.2 us
  starting transfers between devices  23.2 us (24%)
  blocking collectives  18.1 us (19%)
  local copies, waits for them, and re-layouts  16.5 us (17%)
  between operations  13.5 us (14%)
  waiting for transfers between devices  10.5 us (11%)
  matrix products  9.7 us (10%)
  other arithmetic  2.62 us (3%)
    unnamed x11, local copies, waits for them, and re-layouts  9.81 us
    all_gather x1, blocking collectives, per_device(): lax.all_gather(got_rows[None], 'dp', axis=0, tiled=True)  7.51 us
    all_to_all x1, starting transfers between devices, per_device(): lax.all_to_all(send_ten, 'expert', split_axis=0, concat_axis=0, tiled=True)  6.35 us
    all_to_all x1, waiting for transfers between devices, per_device(): lax.all_to_all(home_rows, 'expert', split_axis=1, concat_axis=0, tiled=True)  5.74 us
    all_gather x1, blocking collectives, per_device(): lax.all_gather(got_ten[None], 'dp', axis=0, tiled=True)  5.35 us
    all_gather x1, blocking collectives, per_device(): lax.all_gather(hidden, 'dp', axis=1, tiled=True)  5.24 us
    all_to_all x1, starting transfers between devices, per_device(): lax.all_to_all(home_rows, 'expert', split_axis=1, concat_axis=0, tiled=True)  5.1 us
    all_to_all x1, starting transfers between devices, per_device(): lax.all_to_all(send_rows, 'expert', split_axis=0, concat_axis=0, tiled=True)  5.1 us
  transfers between devices with their start and end apart: 6, of which 2 were waited for; matrix products, arithmetic and copies ran while one was open for 23% of the time, Pallas kernels for 0%

commit v1 on v0

--- a/solution.py
+++ b/solution.py
@@ -2,6 +2,12 @@
 import jax.numpy as jnp
 from jax import lax
 from jax.sharding import PartitionSpec as P
+
+
+def trade_parts(x, axis, split, join):
+    pieces = jnp.split(x, lax.axis_size(axis), axis=split)
+    incoming = lax.all_to_all(jnp.stack(pieces), axis, 0, 0)
+    return jnp.concatenate(incoming, axis=join)
 
 
 def slot_tables(routing, experts, capacity):
@@ -67,9 +73,7 @@
         page_pick[:, :, None] * products.reshape(slot_count, page_count, rank_extent), axis=1
     )
     shrink_low = shrink_result.astype(jnp.bfloat16)
-    expand_every_page = lax.all_to_all(
-        adapter_expand, "dp", split_axis=3, concat_axis=1, tiled=True
-    )[0]
+    expand_every_page = trade_parts(adapter_expand, "dp", 3, 1)[0]
     hidden_part = expand_every_page.shape[2]
     expand_matrix = expand_every_page.reshape(tenants * rank_extent, hidden_part)
     spread_rows = (page_pick[:, :, None] * shrink_low.astype(jnp.float32)[:, None, :]).astype(

time: 95 us -> 85.2 us (0.90)
  local copies, waits for them, and re-layouts: 16.5 us -> 5.25 us
  other arithmetic: 2.62 us -> 4.13 us
    unnamed x11 -> x6, local copies, waits for them, and re-layouts: 9.81 us -> 0.02 us
    all_to_all x2 -> x0, local copies, waits for them, and re-layouts: 2.5 us -> none  [per_device(): lax.all_to_all(adapter_expand, 'dp', split_axis=3, concat_axis=1, tiled=T...]
  transfers between devices with their start and end apart: 6 -> 6, of which waited for: 2 -> 3; matrix products, arithmetic and copies ran while one was open for 23% -> 19% of each run, Pallas kernels for 0% -> 0%
where the time goes in v1:
time: 85.2 us; the launch traced here: 84.4 us
  starting transfers between devices  22.5 us (26%)
  blocking collectives  18.1 us (21%)
  between operations  13.5 us (16%)
  waiting for transfers between devices  11.2 us (13%)
  matrix products  9.7 us (11%)
  local copies, waits for them, and re-layouts  5.25 us (6%)
  other arithmetic  4.13 us (5%)
    all_gather x1, blocking collectives, per_device(): lax.all_gather(got_rows[None], 'dp', axis=0, tiled=True)  7.51 us
    all_to_all x1, starting transfers between devices, per_device(): lax.all_to_all(send_ten, 'expert', split_axis=0, concat_axis=0, tiled=True)  6.35 us
    all_to_all x1, waiting for transfers between devices, per_device(): lax.all_to_all(home_rows, 'expert', split_axis=1, concat_axis=0, tiled=True)  5.74 us
    all_gather x1, blocking collectives, per_device(): lax.all_gather(got_ten[None], 'dp', axis=0, tiled=True)  5.35 us
    all_gather x1, blocking collectives, per_device(): lax.all_gather(hidden, 'dp', axis=1, tiled=True)  5.24 us
    all_to_all x1, starting transfers between devices, per_device(): lax.all_to_all(home_rows, 'expert', split_axis=1, concat_axis=0, tiled=True)  5.11 us
    all_to_all x1, starting transfers between devices, per_device(): lax.all_to_all(send_rows, 'expert', split_axis=0, concat_axis=0, tiled=True)  4.39 us
    dot_general x1, matrix products, per_device(): lax.dot_general(slot_input, flat_pages, (((1,), (1,)), ((), ())), preferr...  4.25 us
  transfers between devices with their start and end apart: 6, of which 3 were waited for; matrix products, arithmetic and copies ran while one was open for 19% of the time, Pallas kernels for 0%

profile of v1, /device:TPU:0, one launch (start us, length us, event | category | flops | bytes accessed | tf_op | source)
XLA Modules:
  0.0 84.4 jit_solution(15228823958038971786)
XLA Ops:
  6.5 0.0 copy-start
  6.5 0.0 all-gather.4.cloned.1.call-start
  6.5 0.7 all-gather.4.cloned.1.call-update
  7.3 0.8 convert_reduce_fusion
  8.1 0.2 reduce_window_sum.11
  8.3 0.7 broadcast_add_fusion
  9.0 0.1 select_reduce_fusion.2
  9.1 0.7 copy.29
  9.8 6.3 %all-to-all-start.1 = ((s32[4,1,2]{2,1,0:T(1,128)}), s32[4,1,2]{2,1,0:T(1,128)S(1)}, u32[]{:S(2)}, u32[]{:S(2)}) async-start(s32[4,1,2]{2,1,0:T(1,128)} %copy.29), calls=%async_computation.1 | async-start | bytes 4096 | tf_op jit(solution)/shard_map/all_to_all | solution.py:48
  16.1 1.0 %convolution_convert_fusion = bf16[4,2,4096]{2,0,1:T(4,128)(2,1)S(1)} fusion(bf16[8,4096]{1,0:T(8,128)(2,1)} %param.10, s32[4,8]{1,0:T(4,128)S(1)} %bitcast.59, pred[4,8]{1,0:T(4,128)(4,1)S(1)} %compare_bitcast_fusion), kind=kOutput, calls=%fused_computation.1 | convolution fusion | flops 557184 | bytes 131232 | tf_op jit(solution)/shard_map/ect,td->ecd/dot_general | solution.py:42
  17.1 0.7 copy.28
  17.8 0.7 dynamic-slice_bitcast_fusion
  18.5 0.9 %slice_bitcast_fusion.3 = (bf16[1,1,6,16,256]{4,3,2,1,0:T(8,128)(2,1)S(1)}, bf16[1,1,6,16,256]{4,3,2,1,0:T(8,128)(2,1)S(1)}, bf16[1,1,6,16,256]{4,3,2,1,0:T(8,128)(2,1)S(1)}, bf16[1,1,6,16,256]{4,3,2,1,0:T(8,128)(2,1)S(1)}) fusion(bf16[1,6,16,1024]{3,2,1,0:T(8,128)(2,1)} %param.19), kind=kLoop, calls=%fused_computation.24 | loop fusion | bytes 393216 | tf_op jit(solution)/shard_map/stack | solution.py:9
  19.4 0.7 pad_maximum_fusion
  20.1 0.7 multiply_select_fusion
  20.9 0.7 all-to-all-done.1
  21.5 4.4 %all-to-all-start = ((bf16[4,2,4096]{2,1,0:T(2,128)(2,1)}), bf16[4,2,4096]{2,1,0:T(2,128)(2,1)S(1)}, u32[]{:S(2)}, u32[]{:S(2)}) async-start(bf16[4,2,4096]{2,1,0:T(2,128)(2,1)} %copy.28), calls=%async_computation | async-start | bytes 131072 | tf_op jit(solution)/shard_map/all_to_all | solution.py:47
  25.9 5.3 %all-gather.1 = s32[16,1,2]{2,1,0:T(1,128)S(1)} all-gather(s32[4,1,2]{2,1,0:T(1,128)S(1)} %all-to-all-done.1), channel_id=3, replica_groups=mesh['group'=2,'expert'=4,'dp'=4] {'dp'}, dimensions={0}, use_global_device_ids=true | all-gather | bytes 160 | tf_op jit(solution)/shard_map/all_gather | solution.py:52
  31.3 0.6 broadcast.74
  31.9 0.7 reduce.3
  32.5 0.1 eq.93
  32.6 0.1 select_reduce_fusion.1
  32.7 0.0 all-to-all-done
  32.7 3.4 %all-to-all-start.2 = ((bf16[4,1,6,16,256]{4,3,2,1,0:T(8,128)(2,1)}), bf16[4,1,6,16,256]{4,3,2,1,0:T(8,128)(2,1)S(1)}, u32[]{:S(2)}, u32[]{:S(2)}) async-start(bf16[4,1,6,16,256]{4,3,2,1,0:T(8,128)(2,1)} %pad_maximum_fusion), calls=%async_computation.2 | async-start | bytes 393216 | tf_op jit(solution)/shard_map/all_to_all | solution.py:9
  36.1 7.5 %all-gather = bf16[16,2,4096]{2,1,0:T(2,128)(2,1)S(1)} all-gather(bf16[4,2,4096]{2,1,0:T(2,128)(2,1)S(1)} %all-to-all-done), channel_id=2, replica_groups=mesh['group'=2,'expert'=4,'dp'=4] {'dp'}, dimensions={0}, use_global_device_ids=true | all-gather | bytes 327680 | tf_op jit(solution)/shard_map/all_gather | solution.py:51
  43.6 0.1 reshape.108
  43.7 0.1 reshape.100
  43.8 0.0 copy-start.1
  43.9 2.2 %fusion.5 = f32[32,256]{1,0:T(8,128)S(1)} fusion(bf16[32,4096]{1,0:T(8,128)(2,1)S(1)} %reshape.100, bf16[1,4096,256]{2,1,0:T(8,128)(2,1)} %param.16), kind=kOutput, calls=%fused_computation.7 | convolution fusion | flops 67108864 | bytes 2392064 | tf_op jit(solution)/shard_map/dot_general | solution.py:86
  46.1 0.0 copy-done.1
  46.1 0.5 fusion.7
  46.5 0.0 all-gather.4.cloned.1.call-done
  46.6 4.2 %fusion.16 = bf16[32,16]{0,1:T(8,128)(2,1)S(1)} fusion(bf16[32,4096,1]{1,0,2:T(8,128)(2,1)S(1)} %reshape.108, bf16[1,24,16,4096]{3,2,0,1:T(8,128)(2,1)} %all-gather.4.cloned.1.call-done, f32[32,24]{0,1:T(8,128)S(1)} %fusion.27), kind=kOutput, calls=%fused_computation.14 | convolution fusion | flops 100687360 | bytes 3411968 | tf_op jit(solution)/shard_map/dot_general | solution.py:69
  50.8 0.0 copy-start.2
  50.9 0.0 all-to-all-done.2
  50.9 0.2 fusion.20
  51.1 5.2 %all_gather.15 = bf16[32,1024]{1,0:T(8,128)(2,1)S(1)} all-gather(bf16[32,256]{1,0:T(8,128)(2,1)S(1)} %fusion.20), channel_id=1, replica_groups=mesh['group'=2,'expert'=4,'dp'=4] {'dp'}, dimensions={1}, use_global_device_ids=true | all-gather | bytes 81920 | tf_op jit(solution)/shard_map/all_gather | solution.py:91
  56.3 0.0 copy-done
  56.3 0.5 fusion.13
  56.8 0.7 reshape.101
  57.5 3.3 %all-to-all-start.3 = ((bf16[4,4,2,1024]{3,2,1,0:T(2,128)(2,1)}), bf16[4,4,2,1024]{3,2,1,0:T(2,128)(2,1)S(1)}, u32[]{:S(2)}, u32[]{:S(2)}) async-start(bf16[4,4,2,1024]{3,2,1,0:T(2,128)(2,1)} %reshape.101), calls=%async_computation.3 | async-start | bytes 131072 | tf_op jit(solution)/shard_map/all_to_all | solution.py:96
  60.8 0.0 copy-done.2
  60.8 0.1 select_reduce_fusion
  60.9 4.0 %all-to-all-done.3 = bf16[4,4,2,1024]{3,2,1,0:T(2,128)(2,1)S(1)} async-done(((bf16[4,4,2,1024]{3,2,1,0:T(2,128)(2,1)}), bf16[4,4,2,1024]{3,2,1,0:T(2,128)(2,1)S(1)}, u32[]{:S(2)}, u32[]{:S(2)}) %all-to-all-start.3) | async-done | bytes 65568 | tf_op jit(solution)/shard_map/all_to_all | solution.py:96
  64.9 0.7 copy.35
  65.5 5.1 %all-to-all-start.4 = ((bf16[1,4,2,4096]{3,2,0,1:T(2,128)(2,1)}), bf16[1,4,2,4096]{3,2,0,1:T(2,128)(2,1)S(1)}, u32[]{:S(2)}, u32[]{:S(2)}) async-start(bf16[1,4,2,4096]{3,2,0,1:T(2,128)(2,1)} %bitcast.18), calls=%async_computation.4 | async-start | bytes 131072 | tf_op jit(solution)/shard_map/all_to_all | solution.py:97
  70.7 5.7 %all-to-all-done.4 = bf16[1,4,2,4096]{3,2,0,1:T(2,128)(2,1)S(1)} async-done(((bf16[1,4,2,4096]{3,2,0,1:T(2,128)(2,1)}), bf16[1,4,2,4096]{3,2,0,1:T(2,128)(2,1)S(1)}, u32[]{:S(2)}, u32[]{:S(2)}) %all-to-all-start.4) | async-done | bytes 65568 | tf_op jit(solution)/shard_map/all_to_all | solution.py:97
  76.4 1.1 %fusion.9 = bf16[8,4096]{1,0:T(8,128)(2,1)} fusion(bf16[8,4096,1]{1,0,2:T(8,128)(2,1)S(1)} %reshape.109, f32[8,8]{1,0:T(8,128)S(1)} %get-tuple-element.5, s32[8,8]{1,0:T(8,128)S(1)} %multiply_add_fusion, pred[8,8]{1,0:T(8,128)(4,1)S(1)} %get-tuple-element.6), kind=kOutput, calls=%fused_computation.11 | convolution fusion | flops 4686848 | bytes 131648 | tf_op jit(solution)/shard_map/tkm,md->tkd/dot_general | solution.py:106
  (10 shorter events, 0.1 us)
Async XLA Ops:
  6.5 49.8 %copy-start = (bf16[1,1024,1024]{2,1,0:T(8,128)(2,1)S(1)}, bf16[1,1024,1024]{2,1,0:T(8,128)(2,1)}, u32[]{:S(2)}) copy-start(bf16[1,1024,1024]{2,1,0:T(8,128)(2,1)} %param.17) | copy-start | bytes 6291460
  6.5 40.0 %all-gather.4.cloned.1.call-start = ((), (), s32[]{:S(2)}) async-start(), calls=%async_computation.5 | async-start | bytes 3932160 | tf_op jit(solution)/shard_map/all_gather | solution.py:66
  9.8 11.8 %all-to-all-start.1 = ((s32[4,1,2]{2,1,0:T(1,128)}), s32[4,1,2]{2,1,0:T(1,128)S(1)}, u32[]{:S(2)}, u32[]{:S(2)}) async-start(s32[4,1,2]{2,1,0:T(1,128)} %copy.29), calls=%async_computation.1 | async-start | bytes 4096 | tf_op jit(solution)/shard_map/all_to_all | solution.py:48
  21.5 11.2 %all-to-all-start = ((bf16[4,2,4096]{2,1,0:T(2,128)(2,1)}), bf16[4,2,4096]{2,1,0:T(2,128)(2,1)S(1)}, u32[]{:S(2)}, u32[]{:S(2)}) async-start(bf16[4,2,4096]{2,1,0:T(2,128)(2,1)} %copy.28), calls=%async_computation | async-start | bytes 131072 | tf_op jit(solution)/shard_map/all_to_all | solution.py:47
  32.7 18.2 %all-to-all-start.2 = ((bf16[4,1,6,16,256]{4,3,2,1,0:T(8,128)(2,1)}), bf16[4,1,6,16,256]{4,3,2,1,0:T(8,128)(2,1)S(1)}, u32[]{:S(2)}, u32[]{:S(2)}) async-start(bf16[4,1,6,16,256]{4,3,2,1,0:T(8,128)(2,1)} %pad_maximum_fusion), calls=%async_computation.2 | async-start | bytes 393216 | tf_op jit(solution)/shard_map/all_to_all | solution.py:9
  43.8 2.2 %copy-start.1 = (bf16[1,4096,256]{2,1,0:T(8,128)(2,1)S(1)}, bf16[1,4096,256]{2,1,0:T(8,128)(2,1)}, u32[]{:S(2)}) copy-start(bf16[1,4096,256]{2,1,0:T(8,128)(2,1)} %param.15) | copy-start | bytes 6291460
  50.8 10.0 %copy-start.2 = (s32[8,8]{1,0:T(8,128)S(1)}, s32[8,8]{1,0:T(8,128)}, u32[]{:S(2)}) copy-start(s32[8,8]{1,0:T(8,128)} %param.11) | copy-start | bytes 772
  57.5 7.4 %all-to-all-start.3 = ((bf16[4,4,2,1024]{3,2,1,0:T(2,128)(2,1)}), bf16[4,4,2,1024]{3,2,1,0:T(2,128)(2,1)S(1)}, u32[]{:S(2)}, u32[]{:S(2)}) async-start(bf16[4,4,2,1024]{3,2,1,0:T(2,128)(2,1)} %reshape.101), calls=%async_computation.3 | async-start | bytes 131072 | tf_op jit(solution)/shard_map/all_to_all | solution.py:96
  65.5 10.9 %all-to-all-start.4 = ((bf16[1,4,2,4096]{3,2,0,1:T(2,128)(2,1)}), bf16[1,4,2,4096]{3,2,0,1:T(2,128)(2,1)S(1)}, u32[]{:S(2)}, u32[]{:S(2)}) async-start(bf16[1,4,2,4096]{3,2,0,1:T(2,128)(2,1)} %bitcast.18), calls=%async_computation.4 | async-start | bytes 131072 | tf_op jit(solution)/shard_map/all_to_all | solution.py:97
Sparse Core Ops, SparseCore 0:
  8.9 31.2 all-gather.3
